TPU v7x, 512 devices: a whole 4x4x16 slice. The times are simulated.
512 devices in a mesh: gx: 8 (over y, core), gy: 4 (over x), gz: 16 (over z).
Axes of the slice: x: 4, y: 4, z: 16, core: 2. Of those that a mesh axis runs over, the one named last changes fastest.
Arguments:
- level_set: float32 [128, 64, 2048], P('gx', 'gy', 'gz'), may hold values from 0 to 1
- velocity: float32 [3, 128, 64, 2048], P(None, 'gx', 'gy', 'gz'), may hold values from -6 to 6
- source: float32 [128, 64, 2048], P('gx', 'gy', 'gz'), may hold values from -6 to 6
- coarse_factor: float32 [512, 512], P(('gx', 'gy', 'gz')), may hold values from -0.2 to 0.2
Outputs:
- level_set_new: float32 [128, 64, 2048], P('gx', 'gy', 'gz')
- pressure: float32 [128, 64, 2048], P('gx', 'gy', 'gz')
All inputs are finite; a program needn't handle non-finite values.
Results may differ from a plain program's by a relative error of at most 0.029.
Values sent between devices are 32-bit elements; how exact they have to be, the bound alone decides.
A program may use at most 64 MiB of HBM per device.

v0:
```python
import jax
import jax.numpy as jnp
import numpy as np
from jax import lax
from jax.sharding import PartitionSpec as P

NP = 8
RSWEEPS = 2
ITERS = 6
GLL_POINTS = (
    -1.0,
    -0.8717401485096066,
    -0.5917001814331423,
    -0.2092992179024789,
    0.2092992179024789,
    0.5917001814331423,
    0.8717401485096066,
    1.0,
)
GLL_WEIGHTS = (
    0.03571428571428571,
    0.21070422714350603,
    0.3411226924835044,
    0.4124587946587038,
    0.4124587946587038,
    0.3411226924835044,
    0.21070422714350603,
    0.03571428571428571,
)
HIGHEST = lax.Precision.HIGHEST
TIME_STEP = 0.02
PSEUDO_STEP = 0.004
INTERFACE_WIDTH = 0.5
GAS_DENSITY = 0.1
SOURCE_SCALE = 20.0


def extended(cells, sides, width):
    for axis, dim in sides:
        count = lax.axis_size(axis)
        ends = count - 1
        head = lax.slice_in_dim(cells, 0, width, axis=dim)
        tail = lax.slice_in_dim(cells, cells.shape[dim] - width, cells.shape[dim], axis=dim)
        cells = jnp.concatenate(
            [
                lax.ppermute(tail, axis, [(i, (i + 1) % count) for i in range(ends)]),
                cells,
                lax.ppermute(head, axis, [((i + 1) % count, i) for i in range(ends)]),
            ],
            axis=dim,
        )
    return cells


def node_tables():
    points = np.array(GLL_POINTS)
    amount = points.shape[0]
    barycentric = np.ones(amount)
    for target in range(amount):
        for partner in range(amount):
            if partner != target:
                barycentric[target] = barycentric[target] / (points[target] - points[partner])
    derivative = np.zeros((amount, amount))
    for target in range(amount):
        for partner in range(amount):
            if partner != target:
                derivative[target, partner] = (
                    barycentric[partner] / barycentric[target] / (points[target] - points[partner])
                )
        derivative[target, target] = -np.sum(derivative[target])
    return derivative


def apply_axis(values, matrix, which_axis):
    if which_axis == 0:
        return jnp.einsum("ap,pqr->aqr", matrix, values, precision=HIGHEST)
    if which_axis == 1:
        return jnp.einsum("aq,pqr->par", matrix, values, precision=HIGHEST)
    return jnp.einsum("pqr,ar->pqa", values, matrix, precision=HIGHEST)


def edge_passes(padded):
    summed = padded
    for which_axis in (1, 2, 3):
        amount = summed.shape[which_axis] - 2
        center = lax.slice_in_dim(summed, 1, amount + 1, axis=which_axis)
        upper_side = lax.slice_in_dim(summed, 2, amount + 2, axis=which_axis)
        lower_side = lax.slice_in_dim(summed, 0, amount, axis=which_axis)
        shape_list = [1, 1, 1, 1]
        shape_list[which_axis] = amount
        position = (jnp.arange(amount) % NP).reshape(shape_list)
        summed = (
            center
            + jnp.where(position == NP - 1, upper_side, 0.0)
            + jnp.where(position == 0, lower_side, 0.0)
        )
    return summed


def assemble(stacked):
    padded = extended(stacked, (("gx", 1), ("gy", 2), ("gz", 3)), 1)
    return edge_passes(padded)


def body(level_set, velocity, source, coarse_factor):
    shape_tuple = level_set.shape
    derivative = node_tables()
    deriv_tables = [
        jnp.asarray(np.kron(np.eye(extent // NP), derivative), jnp.float32)
        for extent in shape_tuple
    ]
    trans_tables = [
        jnp.asarray(np.kron(np.eye(extent // NP), derivative.T), jnp.float32)
        for extent in shape_tuple
    ]
    square_tables = [
        jnp.asarray(np.kron(np.eye(extent // NP), (derivative * derivative).T), jnp.float32)
        for extent in shape_tuple
    ]
    weights = jnp.asarray(np.array(GLL_WEIGHTS), jnp.float32)
    along_x = jnp.tile(weights, shape_tuple[0] // NP)
    along_y = jnp.tile(weights, shape_tuple[1] // NP)
    along_z = jnp.tile(weights, shape_tuple[2] // NP)
    bmass = along_x[:, None, None] * along_y[None, :, None] * along_z[None, None, :]
    gradient = [
        apply_axis(level_set, deriv_tables[which_axis], which_axis) for which_axis in range(3)
    ]
    advect = velocity[0] * gradient[0] + velocity[1] * gradient[1] + velocity[2] * gradient[2]
    divergence = (
        apply_axis(bmass * velocity[0], trans_tables[0], 0)
        + apply_axis(bmass * velocity[1], trans_tables[1], 1)
        + apply_axis(bmass * velocity[2], trans_tables[2], 2)
        + bmass * source
    )
    assembled = assemble(jnp.stack([bmass * advect, bmass, divergence]))
    mass_sum = assembled[1]
    weight = bmass / mass_sum
    level_now = level_set - TIME_STEP * assembled[0] / mass_sum
    rhs_field = SOURCE_SCALE * assembled[2]
    for sweep in range(RSWEEPS):
        gradient = [
            apply_axis(level_now, deriv_tables[which_axis], which_axis) for which_axis in range(3)
        ]
        inv_norm = 1.0 / jnp.sqrt(
            1.0 + gradient[0] * gradient[0] + gradient[1] * gradient[1] + gradient[2] * gradient[2]
        )
        compress = level_now * (1.0 - level_now) * inv_norm
        weak_form = apply_axis(
            bmass * (compress * gradient[0] - INTERFACE_WIDTH * gradient[0]), trans_tables[0], 0
        )
        weak_form = weak_form + apply_axis(
            bmass * (compress * gradient[1] - INTERFACE_WIDTH * gradient[1]), trans_tables[1], 1
        )
        weak_form = weak_form + apply_axis(
            bmass * (compress * gradient[2] - INTERFACE_WIDTH * gradient[2]), trans_tables[2], 2
        )
        level_now = level_now + PSEUDO_STEP * assemble(weak_form[None])[0] / mass_sum
    inverse_density = 1.0 / (GAS_DENSITY + (1.0 - GAS_DENSITY) * jnp.clip(level_now, 0.0, 1.0))
    scaled = bmass * inverse_density
    diag_local = (
        apply_axis(scaled, square_tables[0], 0)
        + apply_axis(scaled, square_tables[1], 1)
        + apply_axis(scaled, square_tables[2], 2)
        + bmass
    )
    diagonal = assemble(diag_local[None])[0]
    own_row = coarse_factor[0]

    def precondition(residual):
        jacobi = residual / diagonal
        restricted = jnp.sum(weight * residual)
        coarse_mid = lax.psum(restricted * own_row, ("gx", "gy", "gz"))
        coarse_value = jnp.dot(own_row, coarse_mid, precision=HIGHEST)
        result = jacobi + assemble((weight * coarse_value)[None])[0]
        return (result, lax.psum(jnp.sum(weight * residual * result), ("gx", "gy", "gz")))

    pressure = jnp.zeros_like(rhs_field)
    residual = rhs_field
    direction, inner_now = precondition(residual)
    for step in range(ITERS):
        local_part = bmass * direction
        for element_which_axis in range(3):
            local_part = local_part + apply_axis(
                scaled
                * apply_axis(direction, deriv_tables[element_which_axis], element_which_axis),
                trans_tables[element_which_axis],
                element_which_axis,
            )
        image = assemble(local_part[None])[0]
        curvature = lax.psum(jnp.sum(weight * direction * image), ("gx", "gy", "gz"))
        step_size = inner_now / curvature
        pressure = pressure + step_size * direction
        residual = residual - step_size * image
        if step + 1 < ITERS:
            preconditioned, inner_next = precondition(residual)
            direction = preconditioned + inner_next / inner_now * direction
            inner_now = inner_next
    return (level_now, pressure)


def solution(mesh):
    in_specs = (
        P("gx", "gy", "gz"),
        P(None, "gx", "gy", "gz"),
        P("gx", "gy", "gz"),
        P(("gx", "gy", "gz"), None),
    )
    out_specs = (P("gx", "gy", "gz"), P("gx", "gy", "gz"))
    return jax.shard_map(body, mesh=mesh, in_specs=in_specs, out_specs=out_specs, check_vma=False)
```

profile of v0, /device:TPU:1, one launch (start us, length us, event | category | flops | bytes accessed | tf_op | source)
XLA Modules:
  0.0 2206.5 jit_solution(12459862347474892173)
XLA Ops:
  6.2 4.6 collective-permute-start
  10.8 5.5 collective-permute-start.1
  20.4 3.9 collective-permute-done.3
  37.9 4.1 collective-permute-start.6
  63.5 5.4 collective-permute-done.11
  87.6 4.9 collective-permute-start.16
  103.5 104.3 %psum.126 = f32[512]{0:T(512)S(1)} all-reduce(f32[512]{0:T(512)S(1)} %broadcast_multiply_fusion.13), channel_id=1, replica_groups=mesh['gx'=8,'gy'=4,'gz'=16] {'gx','gy','gz'}, use_global_device_ids=true, to_apply=%region_1.2 | all-reduce | flops 512 | bytes 4096 | tf_op jit(solution)/shard_map/psum | solution.py:172
  223.2 4.0 collective-permute-start.20
  240.6 4.4 collective-permute-done.23
  256.2 4.3 collective-permute-start.32
  273.4 4.8 collective-permute-done.35
  279.6 104.5 %all-reduce = (f32[]{:T(128)}, f32[]{:T(128)}) all-reduce(f32[]{:T(128)} %get-tuple-element.9, f32[]{:T(128)} %get-tuple-element.8), channel_id=1, replica_groups=mesh['gx'=8,'gy'=4,'gz'=16] {'gx','gy','gz'}, use_global_device_ids=true, to_apply=%region_3.4 | all-reduce | flops 2 | bytes 16 | tf_op jit(solution)/shard_map/psum | solution.py:175
  386.8 98.4 %psum.129 = f32[512]{0:T(512)S(1)} all-reduce(f32[512]{0:T(512)S(1)} %broadcast_multiply_fusion.12), channel_id=1, replica_groups=mesh['gx'=8,'gy'=4,'gz'=16] {'gx','gy','gz'}, use_global_device_ids=true, to_apply=%region_7.8 | all-reduce | flops 512 | bytes 4096 | tf_op jit(solution)/shard_map/psum | solution.py:172
  509.2 3.9 collective-permute-done.41
  514.5 101.3 %psum.130 = f32[]{:T(128)} all-reduce(f32[]{:T(128)} %get-tuple-element.36), channel_id=1, replica_groups=mesh['gx'=8,'gy'=4,'gz'=16] {'gx','gy','gz'}, use_global_device_ids=true, to_apply=%region_9.10 | all-reduce | flops 1 | bytes 8 | tf_op jit(solution)/shard_map/psum | solution.py:175
  645.7 102.2 %psum.131 = f32[]{:T(128)} all-reduce(f32[]{:T(128)} %get-tuple-element.34), channel_id=1, replica_groups=mesh['gx'=8,'gy'=4,'gz'=16] {'gx','gy','gz'}, use_global_device_ids=true, to_apply=%region_11.12 | all-reduce | flops 1 | bytes 8 | tf_op jit(solution)/shard_map/psum | solution.py:190
  750.5 99.1 %psum.132 = f32[512]{0:T(512)S(1)} all-reduce(f32[512]{0:T(512)S(1)} %broadcast_multiply_fusion.11), channel_id=1, replica_groups=mesh['gx'=8,'gy'=4,'gz'=16] {'gx','gy','gz'}, use_global_device_ids=true, to_apply=%region_13.14 | all-reduce | flops 512 | bytes 4096 | tf_op jit(solution)/shard_map/psum | solution.py:172
  874.0 3.9 collective-permute-done.53
  879.3 100.7 %psum.133 = f32[]{:T(128)} all-reduce(f32[]{:T(128)} %get-tuple-element.30), channel_id=1, replica_groups=mesh['gx'=8,'gy'=4,'gz'=16] {'gx','gy','gz'}, use_global_device_ids=true, to_apply=%region_15.16 | all-reduce | flops 1 | bytes 8 | tf_op jit(solution)/shard_map/psum | solution.py:175
  1009.8 102.3 %psum.134 = f32[]{:T(128)} all-reduce(f32[]{:T(128)} %get-tuple-element.28), channel_id=1, replica_groups=mesh['gx'=8,'gy'=4,'gz'=16] {'gx','gy','gz'}, use_global_device_ids=true, to_apply=%region_17.18 | all-reduce | flops 1 | bytes 8 | tf_op jit(solution)/shard_map/psum | solution.py:190
  1114.7 98.7 %psum.135 = f32[512]{0:T(512)S(1)} all-reduce(f32[512]{0:T(512)S(1)} %broadcast_multiply_fusion.10), channel_id=1, replica_groups=mesh['gx'=8,'gy'=4,'gz'=16] {'gx','gy','gz'}, use_global_device_ids=true, to_apply=%region_19.20 | all-reduce | flops 512 | bytes 4096 | tf_op jit(solution)/shard_map/psum | solution.py:172
  1237.8 3.9 collective-permute-done.65
  1243.1 100.7 %psum.136 = f32[]{:T(128)} all-reduce(f32[]{:T(128)} %get-tuple-element.24), channel_id=1, replica_groups=mesh['gx'=8,'gy'=4,'gz'=16] {'gx','gy','gz'}, use_global_device_ids=true, to_apply=%region_21.22 | all-reduce | flops 1 | bytes 8 | tf_op jit(solution)/shard_map/psum | solution.py:175
  1373.6 102.5 %psum.137 = f32[]{:T(128)} all-reduce(f32[]{:T(128)} %get-tuple-element.22), channel_id=1, replica_groups=mesh['gx'=8,'gy'=4,'gz'=16] {'gx','gy','gz'}, use_global_device_ids=true, to_apply=%region_23.24 | all-reduce | flops 1 | bytes 8 | tf_op jit(solution)/shard_map/psum | solution.py:190
  1478.7 98.7 %psum.138 = f32[512]{0:T(512)S(1)} all-reduce(f32[512]{0:T(512)S(1)} %broadcast_multiply_fusion.9), channel_id=1, replica_groups=mesh['gx'=8,'gy'=4,'gz'=16] {'gx','gy','gz'}, use_global_device_ids=true, to_apply=%region_25.26 | all-reduce | flops 512 | bytes 4096 | tf_op jit(solution)/shard_map/psum | solution.py:172
  1601.8 3.9 collective-permute-done.77
  1607.0 100.7 %psum.139 = f32[]{:T(128)} all-reduce(f32[]{:T(128)} %get-tuple-element.18), channel_id=1, replica_groups=mesh['gx'=8,'gy'=4,'gz'=16] {'gx','gy','gz'}, use_global_device_ids=true, to_apply=%region_27.28 | all-reduce | flops 1 | bytes 8 | tf_op jit(solution)/shard_map/psum | solution.py:175
  1737.5 102.3 %psum.140 = f32[]{:T(128)} all-reduce(f32[]{:T(128)} %get-tuple-element.16), channel_id=1, replica_groups=mesh['gx'=8,'gy'=4,'gz'=16] {'gx','gy','gz'}, use_global_device_ids=true, to_apply=%region_29.30 | all-reduce | flops 1 | bytes 8 | tf_op jit(solution)/shard_map/psum | solution.py:190
  1842.5 98.7 %psum.141 = f32[512]{0:T(512)S(1)} all-reduce(f32[512]{0:T(512)S(1)} %broadcast_multiply_fusion.8), channel_id=1, replica_groups=mesh['gx'=8,'gy'=4,'gz'=16] {'gx','gy','gz'}, use_global_device_ids=true, to_apply=%region_31.32 | all-reduce | flops 512 | bytes 4096 | tf_op jit(solution)/shard_map/psum | solution.py:172
  1965.6 3.9 collective-permute-done.89
  1970.8 100.7 %psum.142 = f32[]{:T(128)} all-reduce(f32[]{:T(128)} %get-tuple-element.12), channel_id=1, replica_groups=mesh['gx'=8,'gy'=4,'gz'=16] {'gx','gy','gz'}, use_global_device_ids=true, to_apply=%region_33.34 | all-reduce | flops 1 | bytes 8 | tf_op jit(solution)/shard_map/psum | solution.py:175
  2102.2 102.1 %psum.143 = f32[]{:T(128)} all-reduce(f32[]{:T(128)} %fusion.92), channel_id=1, replica_groups=mesh['gx'=8,'gy'=4,'gz'=16] {'gx','gy','gz'}, use_global_device_ids=true, to_apply=%region_35.36 | all-reduce | flops 1 | bytes 8 | tf_op jit(solution)/shard_map/psum | solution.py:190
  (429 shorter events, 405.3 us)
Async XLA Ops:
  6.2 10.1 collective-permute-start
  54.7 8.8 collective-permute-start.10
  58.3 10.6 collective-permute-start.11
  87.6 10.1 collective-permute-start.16
  92.5 9.1 collective-permute-start.17
  209.1 10.4 collective-permute-start.24
  211.1 8.4 collective-permute-start.25
  214.4 8.8 collective-permute-start.18
  219.6 9.2 collective-permute-start.26
  223.2 8.3 collective-permute-start.20
  228.9 8.1 collective-permute-start.28
  230.2 8.5 collective-permute-start.29
  231.8 8.8 collective-permute-start.22
  235.7 9.3 collective-permute-start.23
  265.1 8.3 collective-permute-start.34
  268.2 10.0 collective-permute-start.35
  500.5 8.7 collective-permute-start.40
  504.2 8.9 collective-permute-start.41
  632.6 7.9 collective-permute-start.46
  635.3 9.1 collective-permute-start.47
  865.3 8.7 collective-permute-start.52
  869.0 8.9 collective-permute-start.53
  999.4 9.1 collective-permute-start.59
  1229.1 8.7 collective-permute-start.64
  1232.8 8.9 collective-permute-start.65
  1363.2 9.1 collective-permute-start.71
  1593.1 8.7 collective-permute-start.76
  1596.8 8.9 collective-permute-start.77
  1727.1 9.1 collective-permute-start.83
  1956.9 8.7 collective-permute-start.88
  1960.6 8.9 collective-permute-start.89
  2091.0 9.1 collective-permute-start.95
  (73 other events, 550.5 us)
where the time goes:
time: 2220 us; the launch traced here: 2210 us
  blocking collectives  1720 us (77%)
  starting transfers between devices  211 us (10%)
  waiting for transfers between devices  199 us (9%)
  other arithmetic  36.4 us (2%)
    psum x6, blocking collectives, precondition(): lax.psum(jnp.sum(weight * residual * result), ('gx', 'gy', 'gz'))  609 us
    psum x6, blocking collectives, precondition(): coarse_mid = lax.psum(restricted * own_row, ('gx', 'gy', 'gz'))  598 us
    psum x5, blocking collectives, body(): lax.psum(jnp.sum(weight * direction * image), ('gx', 'gy', 'gz'))  511 us
    ppermute x48, waiting for transfers between devices, extended(): lax.ppermute(head, axis, [((i + 1) % count, i) for i in range(ends)])  147 us
    ppermute x48, starting transfers between devices, extended(): lax.ppermute(tail, axis, [(i, (i + 1) % count) for i in range(ends)])  133 us
    ppermute x48, starting transfers between devices, extended(): lax.ppermute(head, axis, [((i + 1) % count, i) for i in range(ends)])  77.4 us
    ppermute x48, waiting for transfers between devices, extended(): lax.ppermute(tail, axis, [(i, (i + 1) % count) for i in range(ends)])  51.5 us
  transfers between devices with their start and end apart: 96, of which 59 were waited for; matrix products, arithmetic and copies ran while one was open for 0% of the time, Pallas kernels for 0%

commit v1 on v0

--- a/solution.py
+++ b/solution.py
@@ -169,7 +169,10 @@
     def precondition(residual):
         jacobi = residual / diagonal
         restricted = jnp.sum(weight * residual)
-        coarse_mid = lax.psum(restricted * own_row, ("gx", "gy", "gz"))
+        arrange_the_classes = lambda field_in, a_name: jnp.sum(
+            lax.all_gather(field_in, a_name), axis=0
+        )
+        coarse_mid = arrange_the_classes(restricted * own_row, ("gx", "gy", "gz"))
         coarse_value = jnp.dot(own_row, coarse_mid, precision=HIGHEST)
         result = jacobi + assemble((weight * coarse_value)[None])[0]
         return (result, lax.psum(jnp.sum(weight * residual * result), ("gx", "gy", "gz")))

time: 2220 us -> 2620 us (1.18)
  waiting for transfers between devices: 199 us -> 1160 us
  blocking collectives: 1720 us -> 1120 us
    all_gather x0 -> x6, waiting for transfers between devices: none -> 959 us  [precondition(): lax.all_gather(field_in, a_name)]
    psum x6 -> x0, blocking collectives: 598 us -> none  [precondition(): coarse_mid = lax.psum(restricted * own_row, ('gx', 'gy', 'gz'))]
  transfers between devices with their start and end apart: 96 -> 102, of which waited for: 59 -> 66; matrix products, arithmetic and copies ran while one was open for 0% -> 0% of each run, Pallas kernels for 0% -> 0%
where the time goes in v1:
time: 2620 us; the launch traced here: 2610 us
  waiting for transfers between devices  1160 us (44%)
  blocking collectives  1120 us (43%)
  starting transfers between devices  221 us (8%)
  other arithmetic  50.9 us (2%)
  between operations  31.5 us (1%)
    all_gather x6, waiting for transfers between devices, precondition(): lax.all_gather(field_in, a_name)  959 us
    psum x6, blocking collectives, precondition(): lax.psum(jnp.sum(weight * residual * result), ('gx', 'gy', 'gz'))  607 us
    psum x5, blocking collectives, body(): lax.psum(jnp.sum(weight * direction * image), ('gx', 'gy', 'gz'))  511 us
    ppermute x48, waiting for transfers between devices, extended(): lax.ppermute(head, axis, [((i + 1) % count, i) for i in range(ends)])  149 us
    ppermute x48, starting transfers between devices, extended(): lax.ppermute(tail, axis, [(i, (i + 1) % count) for i in range(ends)])  142 us
    ppermute x48, starting transfers between devices, extended(): lax.ppermute(head, axis, [((i + 1) % count, i) for i in range(ends)])  78 us
    ppermute x48, waiting for transfers between devices, extended(): lax.ppermute(tail, axis, [(i, (i + 1) % count) for i in range(ends)])  52.6 us
  transfers between devices with their start and end apart: 102, of which 66 were waited for; matrix products, arithmetic and copies ran while one was open for 0% of the time, Pallas kernels for 0%

profile of v1, /device:TPU:1, one launch (start us, length us, event | category | flops | bytes accessed | tf_op | source)
XLA Modules:
  0.0 2606.5 jit_solution(18407238822878960591)
XLA Ops:
  12.8 4.6 collective-permute-start
  17.4 5.5 collective-permute-start.1
  27.0 3.9 collective-permute-done.3
  44.4 4.1 collective-permute-start.6
  66.1 3.9 collective-permute-done.10
  70.1 5.4 collective-permute-done.11
  94.2 4.9 collective-permute-start.16
  100.3 3.9 collective-permute-done.16
  123.6 151.8 %all-gather.13.cloned.1.call-done = f32[512,1,512]{2,1,0:T(1,128)} async-done(((f32[1,1,512]{2,1,0:T(1,128)}), f32[512,1,512]{2,1,0:T(1,128)}) %all-gather.13.cloned.1.call-update) | async-done | bytes 1048592 | tf_op jit(solution)/shard_map/all_gather | solution.py:173
  295.9 4.0 collective-permute-start.28
  304.5 4.1 collective-permute-done.29
  311.3 4.0 collective-permute-start.30
  320.3 4.0 collective-permute-start.32
  332.6 3.9 collective-permute-done.34
  341.7 102.6 %all-reduce = (f32[]{:T(128)}, f32[]{:T(128)}) all-reduce(f32[]{:T(128)} %get-tuple-element.9, f32[]{:T(128)} %get-tuple-element.8), channel_id=1, replica_groups=mesh['gx'=8,'gy'=4,'gz'=16] {'gx','gy','gz'}, use_global_device_ids=true, to_apply=%region_3.4 | all-reduce | flops 2 | bytes 16 | tf_op jit(solution)/shard_map/psum | solution.py:178
  447.7 161.5 %all-gather.15.cloned.1.call-done = f32[512,1,512]{2,1,0:T(1,128)} async-done(((f32[1,1,512]{2,1,0:T(1,128)}), f32[512,1,512]{2,1,0:T(1,128)}) %all-gather.15.cloned.1.call-update) | async-done | bytes 1048592 | tf_op jit(solution)/shard_map/all_gather | solution.py:173
  632.4 3.9 collective-permute-done.40
  641.5 100.8 %psum.86 = f32[]{:T(128)} all-reduce(f32[]{:T(128)} %get-tuple-element.36), channel_id=1, replica_groups=mesh['gx'=8,'gy'=4,'gz'=16] {'gx','gy','gz'}, use_global_device_ids=true, to_apply=%region_9.10 | all-reduce | flops 1 | bytes 8 | tf_op jit(solution)/shard_map/psum | solution.py:178
  763.3 3.9 collective-permute-done.46
  772.4 102.2 %psum.87 = f32[]{:T(128)} all-reduce(f32[]{:T(128)} %get-tuple-element.34), channel_id=1, replica_groups=mesh['gx'=8,'gy'=4,'gz'=16] {'gx','gy','gz'}, use_global_device_ids=true, to_apply=%region_11.12 | all-reduce | flops 1 | bytes 8 | tf_op jit(solution)/shard_map/psum | solution.py:193
  877.9 161.6 %all-gather.17.cloned.1.call-done = f32[512,1,512]{2,1,0:T(1,128)} async-done(((f32[1,1,512]{2,1,0:T(1,128)}), f32[512,1,512]{2,1,0:T(1,128)}) %all-gather.17.cloned.1.call-update) | async-done | bytes 1048592 | tf_op jit(solution)/shard_map/all_gather | solution.py:173
  1072.2 100.8 %psum.88 = f32[]{:T(128)} all-reduce(f32[]{:T(128)} %get-tuple-element.30), channel_id=1, replica_groups=mesh['gx'=8,'gy'=4,'gz'=16] {'gx','gy','gz'}, use_global_device_ids=true, to_apply=%region_15.16 | all-reduce | flops 1 | bytes 8 | tf_op jit(solution)/shard_map/psum | solution.py:178
  1203.0 102.2 %psum.89 = f32[]{:T(128)} all-reduce(f32[]{:T(128)} %get-tuple-element.28), channel_id=1, replica_groups=mesh['gx'=8,'gy'=4,'gz'=16] {'gx','gy','gz'}, use_global_device_ids=true, to_apply=%region_17.18 | all-reduce | flops 1 | bytes 8 | tf_op jit(solution)/shard_map/psum | solution.py:193
  1308.5 161.6 %all-gather.19.cloned.1.call-done = f32[512,1,512]{2,1,0:T(1,128)} async-done(((f32[1,1,512]{2,1,0:T(1,128)}), f32[512,1,512]{2,1,0:T(1,128)}) %all-gather.19.cloned.1.call-update) | async-done | bytes 1048592 | tf_op jit(solution)/shard_map/all_gather | solution.py:173
  1502.5 100.8 %psum.90 = f32[]{:T(128)} all-reduce(f32[]{:T(128)} %get-tuple-element.24), channel_id=1, replica_groups=mesh['gx'=8,'gy'=4,'gz'=16] {'gx','gy','gz'}, use_global_device_ids=true, to_apply=%region_21.22 | all-reduce | flops 1 | bytes 8 | tf_op jit(solution)/shard_map/psum | solution.py:178
  1633.4 102.2 %psum.91 = f32[]{:T(128)} all-reduce(f32[]{:T(128)} %get-tuple-element.22), channel_id=1, replica_groups=mesh['gx'=8,'gy'=4,'gz'=16] {'gx','gy','gz'}, use_global_device_ids=true, to_apply=%region_23.24 | all-reduce | flops 1 | bytes 8 | tf_op jit(solution)/shard_map/psum | solution.py:193
  1739.2 161.3 %all-gather.21.cloned.1.call-done = f32[512,1,512]{2,1,0:T(1,128)} async-done(((f32[1,1,512]{2,1,0:T(1,128)}), f32[512,1,512]{2,1,0:T(1,128)}) %all-gather.21.cloned.1.call-update) | async-done | bytes 1048592 | tf_op jit(solution)/shard_map/all_gather | solution.py:173
  1932.9 100.8 %psum.92 = f32[]{:T(128)} all-reduce(f32[]{:T(128)} %get-tuple-element.18), channel_id=1, replica_groups=mesh['gx'=8,'gy'=4,'gz'=16] {'gx','gy','gz'}, use_global_device_ids=true, to_apply=%region_27.28 | all-reduce | flops 1 | bytes 8 | tf_op jit(solution)/shard_map/psum | solution.py:178
  2063.8 102.2 %psum.93 = f32[]{:T(128)} all-reduce(f32[]{:T(128)} %get-tuple-element.16), channel_id=1, replica_groups=mesh['gx'=8,'gy'=4,'gz'=16] {'gx','gy','gz'}, use_global_device_ids=true, to_apply=%region_29.30 | all-reduce | flops 1 | bytes 8 | tf_op jit(solution)/shard_map/psum | solution.py:193
  2169.3 161.6 %all-gather.23.cloned.1.call-done = f32[512,1,512]{2,1,0:T(1,128)} async-done(((f32[1,1,512]{2,1,0:T(1,128)}), f32[512,1,512]{2,1,0:T(1,128)}) %all-gather.23.cloned.1.call-update) | async-done | bytes 1048592 | tf_op jit(solution)/shard_map/all_gather | solution.py:173
  2363.3 100.8 %psum.94 = f32[]{:T(128)} all-reduce(f32[]{:T(128)} %get-tuple-element.12), channel_id=1, replica_groups=mesh['gx'=8,'gy'=4,'gz'=16] {'gx','gy','gz'}, use_global_device_ids=true, to_apply=%region_33.34 | all-reduce | flops 1 | bytes 8 | tf_op jit(solution)/shard_map/psum | solution.py:178
  2494.9 102.2 %psum.95 = f32[]{:T(128)} all-reduce(f32[]{:T(128)} %fusion.92), channel_id=1, replica_groups=mesh['gx'=8,'gy'=4,'gz'=16] {'gx','gy','gz'}, use_global_device_ids=true, to_apply=%region_35.36 | all-reduce | flops 1 | bytes 8 | tf_op jit(solution)/shard_map/psum | solution.py:193
  (447 shorter events, 433.8 us)
Async XLA Ops:
  7.2 268.2 %all-gather.13.cloned.1.call-start = ((), (), s32[]{:S(2)}) async-start(), calls=%async_computation | async-start | bytes 1050624 | tf_op jit(solution)/shard_map/all_gather | solution.py:173
  12.8 10.1 collective-permute-start
  61.3 8.8 collective-permute-start.10
  64.8 10.6 collective-permute-start.11
  94.2 10.1 collective-permute-start.16
  99.0 9.1 collective-permute-start.17
  110.7 498.5 %all-gather.15.cloned.1.call-start = ((), (), s32[]{:S(2)}) async-start(), calls=%async_computation.1 | async-start | bytes 1050624 | tf_op jit(solution)/shard_map/all_gather | solution.py:173
  119.8 164.0 %collective-permute-start.20 = (f32[1,18,1,128]{3,1,2,0:T(8,128)S(1)}, f32[1,18,1,128]{3,1,2,0:T(8,128)S(1)}, u32[]{:S(2)}, u32[]{:S(2)}) collective-permute-start(f32[1,18,1,128]{3,1,2,0:T(8,128)S(1)} %get-tuple-element.111), channel_id=1, source_target_pairs={{0,16},{16,32},{32,48},{1,17},{17,33},{33,49},{2,18},{18,34},{34,5... | collective-permute-start | bytes 27656 | tf_op jit(solution)/shard_map/ppermute | solution.py:46
  122.3 161.6 %collective-permute-start.21 = (f32[1,18,1,128]{3,1,2,0:T(8,128)S(1)}, f32[1,18,1,128]{3,1,2,0:T(8,128)S(1)}, u32[]{:S(2)}, u32[]{:S(2)}) collective-permute-start(f32[1,18,1,128]{3,1,2,0:T(8,128)S(1)} %get-tuple-element.112), channel_id=1, source_target_pairs={{16,0},{32,16},{48,32},{17,1},{33,17},{49,33},{18,2},{34,18},{50,3... | collective-permute-start | bytes 27656 | tf_op jit(solution)/shard_map/ppermute | solution.py:48
  286.9 8.8 collective-permute-start.26
  291.6 9.6 collective-permute-start.22
  294.4 8.2 collective-permute-start.23
  295.9 8.6 collective-permute-start.28
  299.9 8.7 collective-permute-start.29
  331.3 9.1 collective-permute-start.35
  447.6 591.9 %all-gather.17.cloned.1.call-start = ((), (), s32[]{:S(2)}) async-start(), calls=%async_computation.2 | async-start | bytes 1050624 | tf_op jit(solution)/shard_map/all_gather | solution.py:173
  631.1 9.1 collective-permute-start.41
  762.0 9.1 collective-permute-start.47
  877.9 592.2 %all-gather.19.cloned.1.call-start = ((), (), s32[]{:S(2)}) async-start(), calls=%async_computation.3 | async-start | bytes 1050624 | tf_op jit(solution)/shard_map/all_gather | solution.py:173
  1061.7 9.1 collective-permute-start.53
  1192.6 9.1 collective-permute-start.59
  1308.5 592.0 %all-gather.21.cloned.1.call-start = ((), (), s32[]{:S(2)}) async-start(), calls=%async_computation.4 | async-start | bytes 1050624 | tf_op jit(solution)/shard_map/all_gather | solution.py:173
  1489.3 8.0 collective-permute-start.64
  1492.1 9.1 collective-permute-start.65
  1623.0 9.1 collective-permute-start.71
  1738.9 592.0 %all-gather.23.cloned.1.call-start = ((), (), s32[]{:S(2)}) async-start(), calls=%async_computation.5 | async-start | bytes 1050624 | tf_op jit(solution)/shard_map/all_gather | solution.py:173
  1919.7 8.0 collective-permute-start.76
  1922.5 9.1 collective-permute-start.77
  2053.4 9.1 collective-permute-start.83
  2350.1 8.0 collective-permute-start.88
  2352.9 9.1 collective-permute-start.89
  2483.8 9.1 collective-permute-start.95
  (79 other events, 384.1 us)
Sparse Core Ops, SparseCore 0:
  110.8 164.5 all-gather.12
  447.7 161.3 all-gather.14
  878.0 161.4 all-gather.16
  1308.6 161.4 all-gather.18
  1739.0 161.4 all-gather.20
  2169.4 161.4 all-gather.22
